TPU v7x, 32 devices: a whole 2x2x4 slice. The times are simulated.
32 devices in a mesh: depth: 4 (over z), lat: 8 (over y, x, core).
Axes of the slice: x: 2, y: 2, z: 4, core: 2. Of those that a mesh axis runs over, the one named last changes fastest.
Arguments:
- volume_init: float32 [16, 64, 16, 128], P('depth', 'lat'), may hold values from 0.2 to 10
- measured: float32 [64, 16, 128], P('lat'), may hold values from 0.25 to 4
- psf: bfloat16 [16, 13, 128, 128], P('depth'), may hold values from 0 to 0.0043269231
- offsets: int32 [16, 13], replicated, may hold values from 0 to 24, as said below
- counts: int32 [16], replicated, may hold values from 1 to 13, 130 in all
Outputs:
- volume: float32 [16, 64, 16, 128], P('depth', 'lat')
Inputs may be any that keep to these rules, and one draw needn't show every extreme that they name: `offsets`: entry v names the block offset (v // 5 - 2, v % 5 - 2) in patch rows and patches; the entries of one depth are distinct, and entry 0 of every depth is the central offset 2 * 5 + 2.
All inputs are finite; a program needn't handle non-finite values.
Results may differ from a plain program's by a relative error of at most 0.00076.
Values may be sent and summed in bfloat16 or wider, within the bound.
A program may use at most 64 MiB of HBM per device.

v0:
```python
import jax
import jax.numpy as jnp
from jax import lax
from jax.sharding import PartitionSpec as P

RY = 2
RX = 2
ITERS = 2


def with_halo(cells, sides, width):
    for axis, dim in sides:
        count = lax.axis_size(axis)
        ends = count - 1
        head = lax.slice_in_dim(cells, 0, width, axis=dim)
        tail = lax.slice_in_dim(cells, cells.shape[dim] - width, cells.shape[dim], axis=dim)
        cells = jnp.concatenate(
            [
                lax.ppermute(tail, axis, [(i, (i + 1) % count) for i in range(ends)]),
                cells,
                lax.ppermute(head, axis, [((i + 1) % count, i) for i in range(ends)]),
            ],
            axis=dim,
        )
    return cells


def split_offsets(offsets):
    span_x = 2 * RX + 1
    return (offsets // span_x - RY, offsets % span_x - RX)


def project(plane, blocks, rows_by, cols_by, transpose):
    plane_rows = plane.shape[0]
    plane_cols = plane.shape[1]
    tile_rows = plane_rows - 2 * RY
    tile_cols = plane_cols - 2 * RX
    pixels = plane.shape[2]
    flat_plane = plane.reshape(plane_rows * plane_cols, pixels)
    span_x = 2 * RX + 1
    span_all = (2 * RY + 1) * span_x
    codes = (rows_by + RY) * span_x + (cols_by + RX)
    one_hot = (codes[:, None] == jnp.arange(span_all, dtype=jnp.int32)[None, :]).astype(jnp.float32)
    block_values = blocks.astype(jnp.float32)
    if transpose:
        dense = jnp.einsum("ko,kji->ioj", one_hot, block_values, precision=lax.Precision.HIGHEST)
    else:
        dense = jnp.einsum("ko,kji->joi", one_hot, block_values, precision=lax.Precision.HIGHEST)
    dense = dense.astype(jnp.bfloat16).reshape(pixels, span_all * pixels)
    products = jnp.dot(flat_plane, dense, preferred_element_type=jnp.float32).reshape(
        plane_rows, plane_cols, span_all, pixels
    )
    total = jnp.zeros((tile_rows, tile_cols, pixels), jnp.float32)
    for code in range(span_all):
        row_start = code // span_x
        col_start = code % span_x
        total = (
            total
            + products[row_start : row_start + tile_rows, col_start : col_start + tile_cols, code]
        )
    return total


def shards(volume_init, measured, psf, offsets, counts):
    depth_here = volume_init.shape[0]
    tile_rows = volume_init.shape[1]
    tile_cols = volume_init.shape[2]
    pixels = volume_init.shape[3]
    slot_total = psf.shape[1]
    base_depth = lax.axis_index("depth") * depth_here
    local_offsets = lax.dynamic_slice_in_dim(offsets, base_depth, depth_here, 0)
    local_counts = lax.dynamic_slice_in_dim(counts, base_depth, depth_here, 0)
    slot_ids = jnp.arange(slot_total, dtype=jnp.int32)
    live = slot_ids[None, :] < local_counts[:, None]
    weights = jnp.where(live[:, :, None, None], psf, jnp.zeros_like(psf))
    shift_rows, shift_cols = split_offsets(local_offsets)
    all_rows = tile_rows * lax.axis_size("lat")
    row_ids = lax.axis_index("lat") * tile_rows + jnp.arange(tile_rows, dtype=jnp.int32)
    col_ids = jnp.arange(tile_cols, dtype=jnp.int32)
    coverages = []
    for plane_id in range(depth_here):
        source_rows = row_ids[None, :] - shift_rows[plane_id][:, None]
        source_cols = col_ids[None, :] - shift_cols[plane_id][:, None]
        inside_rows = (source_rows >= 0) & (source_rows < all_rows)
        inside_cols = (source_cols >= 0) & (source_cols < tile_cols)
        inside = (inside_rows[:, :, None] & inside_cols[:, None, :]).astype(jnp.float32)
        column_sums = jnp.sum(weights[plane_id].astype(jnp.float32), axis=2)
        coverages.append(
            jnp.einsum("kyx,kj->yxj", inside, column_sums, precision=lax.Precision.HIGHEST)
        )
    volume = volume_init
    for repeat in range(ITERS):
        extended = with_halo(volume.astype(jnp.bfloat16), (("lat", 1),), RY)
        padded = jnp.pad(extended, ((0, 0), (0, 0), (RX, RX), (0, 0)))
        partial_sensor = jnp.zeros((tile_rows, tile_cols, pixels), jnp.float32)
        for plane_id in range(depth_here):
            partial_sensor = partial_sensor + project(
                padded[plane_id],
                weights[plane_id],
                shift_rows[plane_id],
                shift_cols[plane_id],
                False,
            )
        sensor = lax.psum(partial_sensor, "depth")
        ratio = (measured / sensor).astype(jnp.bfloat16)
        ratio_ext = with_halo(ratio, (("lat", 0),), RY)
        ratio_pad = jnp.pad(ratio_ext, ((0, 0), (RX, RX), (0, 0)))
        updated = []
        for plane_id in range(depth_here):
            back = project(
                ratio_pad, weights[plane_id], -shift_rows[plane_id], -shift_cols[plane_id], True
            )
            updated.append(volume[plane_id] * back / coverages[plane_id])
        volume = jnp.stack(updated)
    return volume


def solution(mesh):
    return jax.shard_map(
        shards,
        mesh=mesh,
        in_specs=(
            P("depth", "lat", None, None),
            P("lat", None, None),
            P("depth", None, None, None),
            P(),
            P(),
        ),
        out_specs=P("depth", "lat", None, None),
        check_vma=False,
    )
```

profile of v0, /device:TPU:3, one launch (start us, length us, event | category | flops | bytes accessed | tf_op | source)
XLA Modules:
  0.0 168.0 jit_solution(4459511551675382461)
XLA Ops:
  6.5 1.0 convert_element_type.60
  7.5 3.7 %collective-permute-start = (bf16[4,2,16,128]{3,2,1,0:T(8,128)(2,1)S(1)}, bf16[4,2,16,128]{3,2,1,0:T(8,128)(2,1)}, u32[]{:S(2)}, u32[]{:S(2)}) collective-permute-start(bf16[4,2,16,128]{3,2,1,0:T(8,128)(2,1)S(1)} %get-tuple-element.19), channel_id=1, source_target_pairs={{0,1},{1,2},{2,3},{3,4},{4,5},{5,6},{6,7},{8,9},{9,10},{10,11},{11... | collective-permute-start | bytes 98312 | tf_op jit(solution)/shard_map/ppermute | solution.py:19
  11.2 1.9 %collective-permute-start.1 = (bf16[4,2,16,128]{3,2,1,0:T(8,128)(2,1)S(1)}, bf16[4,2,16,128]{3,2,1,0:T(8,128)(2,1)}, u32[]{:S(2)}, u32[]{:S(2)}) collective-permute-start(bf16[4,2,16,128]{3,2,1,0:T(8,128)(2,1)S(1)} %get-tuple-element.20), channel_id=1, source_target_pairs={{1,0},{2,1},{3,2},{4,3},{5,4},{6,5},{7,6},{9,8},{10,9},{11,10},{12... | collective-permute-start | bytes 98312 | tf_op jit(solution)/shard_map/ppermute | solution.py:21
  15.3 2.5 %copy_select_fusion = bf16[4,13,128,128]{3,1,2,0:T(8,128)(2,1)S(1)} fusion(bf16[4,13,128,128]{3,2,1,0:T(8,128)(2,1)} %param.7, pred[4,13]{1,0:T(4,128)(4,1)S(1)} %iota_compare_fusion.12), kind=kLoop, calls=%fused_computation | loop fusion | flops 851968 | bytes 3407924 | tf_op jit(solution)/shard_map/jit(_where)/select_n | solution.py:75
  17.8 1.2 convert_reduce_fusion.3
  19.6 1.5 fusion.2
  21.1 1.5 fusion.1
  22.6 1.5 fusion
  24.1 1.5 fusion.4
  26.2 1.5 fusion.5
  28.4 1.5 fusion.6
  30.6 1.5 fusion.7
  35.4 1.2 copy.892
  36.6 2.1 %copy.866 = bf16[128,25,128]{0,2,1:T(8,128)(2,1)S(1)} copy(bf16[128,25,128]{2,1,0:T(8,128)(2,1)} %fusion.2) | data formatting | bytes 1638400 | tf_op jit(solution)/shard_map/convert_element_type | solution.py:49
  38.8 2.1 %copy.840 = bf16[128,25,128]{0,2,1:T(8,128)(2,1)S(1)} copy(bf16[128,25,128]{2,1,0:T(8,128)(2,1)} %fusion.1) | data formatting | bytes 1638400 | tf_op jit(solution)/shard_map/convert_element_type | solution.py:49
  40.9 2.1 %copy.815 = bf16[128,25,128]{0,2,1:T(8,128)(2,1)S(1)} copy(bf16[128,25,128]{2,1,0:T(8,128)(2,1)} %fusion) | data formatting | bytes 1638400 | tf_op jit(solution)/shard_map/convert_element_type | solution.py:49
  46.8 1.2 fusion.221
  48.0 33.3 %all-reduce.7.cloned.1.call-done = f32[8,16,128]{2,1,0:T(8,128)} async-done(((f32[8,16,128]{2,1,0:T(8,128)}), f32[8,16,128]{2,1,0:T(8,128)}) %all-reduce.7.cloned.1.call-update) | async-done | bytes 65552 | tf_op jit(solution)/shard_map/psum | solution.py:104
  81.4 1.0 divide_convert_fusion.1
  82.3 5.6 %collective-permute-start.2 = (bf16[2,16,128]{2,1,0:T(8,128)(2,1)S(1)}, bf16[2,16,128]{2,1,0:T(8,128)(2,1)S(1)}, u32[]{:S(2)}, u32[]{:S(2)}) collective-permute-start(bf16[2,16,128]{2,1,0:T(8,128)(2,1)S(1)} %get-tuple-element.23), channel_id=1, source_target_pairs={{0,1},{1,2},{2,3},{3,4},{4,5},{5,6},{6,7},{8,9},{9,10},{10,11},{11... | collective-permute-start | bytes 24584 | tf_op jit(solution)/shard_map/ppermute | solution.py:19
  88.0 2.1 %collective-permute-start.3 = (bf16[2,16,128]{2,1,0:T(8,128)(2,1)S(1)}, bf16[2,16,128]{2,1,0:T(8,128)(2,1)S(1)}, u32[]{:S(2)}, u32[]{:S(2)}) collective-permute-start(bf16[2,16,128]{2,1,0:T(8,128)(2,1)S(1)} %get-tuple-element.24), channel_id=1, source_target_pairs={{1,0},{2,1},{3,2},{4,3},{5,4},{6,5},{7,6},{9,8},{10,9},{11,10},{12... | collective-permute-start | bytes 24584 | tf_op jit(solution)/shard_map/ppermute | solution.py:21
  90.1 1.1 fusion.275
  91.2 2.7 %collective-permute-done.3 = bf16[2,16,128]{2,1,0:T(8,128)(2,1)S(1)} collective-permute-done((bf16[2,16,128]{2,1,0:T(8,128)(2,1)S(1)}, bf16[2,16,128]{2,1,0:T(8,128)(2,1)S(1)}, u32[]{:S(2)}, u32[]{:S(2)}) %collective-permute-start.3) | collective-permute-done | bytes 8224 | tf_op jit(solution)/shard_map/ppermute | solution.py:21
  93.9 2.0 %fusion.22 = f32[12,20,25,128]{3,1,2,0:T(8,128)S(1)} fusion(bf16[128,25,128]{0,1,2:T(8,128)(2,1)} %fusion.4, bf16[2,16,128]{2,1,0:T(8,128)(2,1)S(1)} %collective-permute-done.3, bf16[8,16,128]{2,1,0:T(8,128)(2,1)S(1)} %divide_convert_fusion.1, bf16[2,16,128]{2,1,0:T(8,128)(2,1)S(1)} %collective-permute-done.2), kind=kOutput, calls=%fused_computation.37 | convolution fusion | flops 196976640 | bytes 3940352 | tf_op jit(solution)/shard_map/dot_general | solution.py:50
  101.3 1.9 %collective-permute-start.4 = (bf16[4,2,16,128]{3,2,1,0:T(8,128)(2,1)S(1)}, bf16[4,2,16,128]{3,2,1,0:T(8,128)(2,1)S(1)}, u32[]{:S(2)}, u32[]{:S(2)}) collective-permute-start(bf16[4,2,16,128]{3,2,1,0:T(8,128)(2,1)S(1)} %get-tuple-element.17), channel_id=1, source_target_pairs={{0,1},{1,2},{2,3},{3,4},{4,5},{5,6},{6,7},{8,9},{9,10},{10,11},{11... | collective-permute-start | bytes 98312 | tf_op jit(solution)/shard_map/ppermute | solution.py:19
  103.3 2.4 %collective-permute-start.5 = (bf16[4,2,16,128]{3,2,1,0:T(8,128)(2,1)S(1)}, bf16[4,2,16,128]{3,2,1,0:T(8,128)(2,1)S(1)}, u32[]{:S(2)}, u32[]{:S(2)}) collective-permute-start(bf16[4,2,16,128]{3,2,1,0:T(8,128)(2,1)S(1)} %get-tuple-element.18), channel_id=1, source_target_pairs={{1,0},{2,1},{3,2},{4,3},{5,4},{6,5},{7,6},{9,8},{10,9},{11,10},{12... | collective-permute-start | bytes 98312 | tf_op jit(solution)/shard_map/ppermute | solution.py:21
  105.7 3.7 %collective-permute-done.5 = bf16[4,2,16,128]{3,2,1,0:T(8,128)(2,1)S(1)} collective-permute-done((bf16[4,2,16,128]{3,2,1,0:T(8,128)(2,1)S(1)}, bf16[4,2,16,128]{3,2,1,0:T(8,128)(2,1)S(1)}, u32[]{:S(2)}, u32[]{:S(2)}) %collective-permute-start.5) | collective-permute-done | bytes 32800 | tf_op jit(solution)/shard_map/ppermute | solution.py:21
  112.3 1.2 fusion.106
  113.6 30.4 %all-reduce.9.cloned.1.call-done = f32[8,16,128]{2,1,0:T(8,128)} async-done(((f32[8,16,128]{2,1,0:T(8,128)}), f32[8,16,128]{2,1,0:T(8,128)}) %all-reduce.9.cloned.1.call-update) | async-done | bytes 65552 | tf_op jit(solution)/shard_map/psum | solution.py:104
  144.9 5.6 %collective-permute-start.6 = (bf16[2,16,128]{2,1,0:T(8,128)(2,1)S(1)}, bf16[2,16,128]{2,1,0:T(8,128)(2,1)S(1)}, u32[]{:S(2)}, u32[]{:S(2)}) collective-permute-start(bf16[2,16,128]{2,1,0:T(8,128)(2,1)S(1)} %get-tuple-element.21), channel_id=1, source_target_pairs={{0,1},{1,2},{2,3},{3,4},{4,5},{5,6},{6,7},{8,9},{9,10},{10,11},{11... | collective-permute-start | bytes 24584 | tf_op jit(solution)/shard_map/ppermute | solution.py:19
  150.5 1.9 %collective-permute-start.7 = (bf16[2,16,128]{2,1,0:T(8,128)(2,1)S(1)}, bf16[2,16,128]{2,1,0:T(8,128)(2,1)S(1)}, u32[]{:S(2)}, u32[]{:S(2)}) collective-permute-start(bf16[2,16,128]{2,1,0:T(8,128)(2,1)S(1)} %get-tuple-element.22), channel_id=1, source_target_pairs={{1,0},{2,1},{3,2},{4,3},{5,4},{6,5},{7,6},{9,8},{10,9},{11,10},{12... | collective-permute-start | bytes 24584 | tf_op jit(solution)/shard_map/ppermute | solution.py:21
  152.5 3.9 %collective-permute-done.7 = bf16[2,16,128]{2,1,0:T(8,128)(2,1)S(1)} collective-permute-done((bf16[2,16,128]{2,1,0:T(8,128)(2,1)S(1)}, bf16[2,16,128]{2,1,0:T(8,128)(2,1)S(1)}, u32[]{:S(2)}, u32[]{:S(2)}) %collective-permute-start.7) | collective-permute-done | bytes 8224 | tf_op jit(solution)/shard_map/ppermute | solution.py:21
  (97 shorter events, 25.4 us)
Async XLA Ops:
  6.5 74.8 %all-reduce.7.cloned.1.call-start = ((), (), s32[]{:S(2)}) async-start(), calls=%async_computation | async-start | bytes 131072 | tf_op jit(solution)/shard_map/psum | solution.py:104
  7.5 35.5 %collective-permute-start = (bf16[4,2,16,128]{3,2,1,0:T(8,128)(2,1)S(1)}, bf16[4,2,16,128]{3,2,1,0:T(8,128)(2,1)}, u32[]{:S(2)}, u32[]{:S(2)}) collective-permute-start(bf16[4,2,16,128]{3,2,1,0:T(8,128)(2,1)S(1)} %get-tuple-element.19), channel_id=1, source_target_pairs={{0,1},{1,2},{2,3},{3,4},{4,5},{5,6},{6,7},{8,9},{9,10},{10,11},{11... | collective-permute-start | bytes 98312 | tf_op jit(solution)/shard_map/ppermute | solution.py:19
  11.2 31.9 %collective-permute-start.1 = (bf16[4,2,16,128]{3,2,1,0:T(8,128)(2,1)S(1)}, bf16[4,2,16,128]{3,2,1,0:T(8,128)(2,1)}, u32[]{:S(2)}, u32[]{:S(2)}) collective-permute-start(bf16[4,2,16,128]{3,2,1,0:T(8,128)(2,1)S(1)} %get-tuple-element.20), channel_id=1, source_target_pairs={{1,0},{2,1},{3,2},{4,3},{5,4},{6,5},{7,6},{9,8},{10,9},{11,10},{12... | collective-permute-start | bytes 98312 | tf_op jit(solution)/shard_map/ppermute | solution.py:21
  48.0 47.9 %copy-start.7 = (f32[4,8,16,128]{3,2,1,0:T(8,128)S(1)}, f32[4,8,16,128]{3,2,1,0:T(8,128)}, u32[]{:S(2)}) copy-start(f32[4,8,16,128]{3,2,1,0:T(8,128)} %param.5) | copy-start | bytes 786436
  48.0 96.1 %all-reduce.9.cloned.1.call-start = ((), (), s32[]{:S(2)}) async-start(), calls=%async_computation.1 | async-start | bytes 131072 | tf_op jit(solution)/shard_map/psum | solution.py:104
  81.3 14.5 %copy-start.12 = (f32[8,16,128]{2,1,0:T(8,128)S(1)}, f32[8,16,128]{2,1,0:T(8,128)}, u32[]{:S(2)}) copy-start(f32[8,16,128]{2,1,0:T(8,128)} %fusion.281) | copy-start | bytes 196612
  81.4 15.3 %copy-start.5 = (bf16[128,25,128]{0,1,2:T(8,128)(2,1)S(1)}, bf16[128,25,128]{0,1,2:T(8,128)(2,1)}, u32[]{:S(2)}) copy-start(bf16[128,25,128]{0,1,2:T(8,128)(2,1)} %fusion.5) | copy-start | bytes 2457604
  82.3 8.8 %collective-permute-start.2 = (bf16[2,16,128]{2,1,0:T(8,128)(2,1)S(1)}, bf16[2,16,128]{2,1,0:T(8,128)(2,1)S(1)}, u32[]{:S(2)}, u32[]{:S(2)}) collective-permute-start(bf16[2,16,128]{2,1,0:T(8,128)(2,1)S(1)} %get-tuple-element.23), channel_id=1, source_target_pairs={{0,1},{1,2},{2,3},{3,4},{4,5},{5,6},{6,7},{8,9},{9,10},{10,11},{11... | collective-permute-start | bytes 24584 | tf_op jit(solution)/shard_map/ppermute | solution.py:19
  88.0 5.9 %collective-permute-start.3 = (bf16[2,16,128]{2,1,0:T(8,128)(2,1)S(1)}, bf16[2,16,128]{2,1,0:T(8,128)(2,1)S(1)}, u32[]{:S(2)}, u32[]{:S(2)}) collective-permute-start(bf16[2,16,128]{2,1,0:T(8,128)(2,1)S(1)} %get-tuple-element.24), channel_id=1, source_target_pairs={{1,0},{2,1},{3,2},{4,3},{5,4},{6,5},{7,6},{9,8},{10,9},{11,10},{12... | collective-permute-start | bytes 24584 | tf_op jit(solution)/shard_map/ppermute | solution.py:21
  91.2 9.3 %copy-start.14 = (f32[8,16,128]{2,1,0:T(8,128)}, f32[8,16,128]{2,1,0:T(8,128)S(1)}, u32[]{:S(2)}) copy-start(f32[8,16,128]{2,1,0:T(8,128)S(1)} %fusion.275) | copy-start | bytes 196612
  95.8 1.6 copy-start.10
  95.8 2.4 %copy-start.3 = (bf16[128,25,128]{0,1,2:T(8,128)(2,1)S(1)}, bf16[128,25,128]{0,1,2:T(8,128)(2,1)}, u32[]{:S(2)}) copy-start(bf16[128,25,128]{0,1,2:T(8,128)(2,1)} %fusion.6) | copy-start | bytes 2457604
  97.4 1.6 copy-start.8
  97.4 2.3 %copy-start.1 = (bf16[128,25,128]{0,1,2:T(8,128)(2,1)S(1)}, bf16[128,25,128]{0,1,2:T(8,128)(2,1)}, u32[]{:S(2)}) copy-start(bf16[128,25,128]{0,1,2:T(8,128)(2,1)} %fusion.7) | copy-start | bytes 2457604
  101.3 4.3 %collective-permute-start.4 = (bf16[4,2,16,128]{3,2,1,0:T(8,128)(2,1)S(1)}, bf16[4,2,16,128]{3,2,1,0:T(8,128)(2,1)S(1)}, u32[]{:S(2)}, u32[]{:S(2)}) collective-permute-start(bf16[4,2,16,128]{3,2,1,0:T(8,128)(2,1)S(1)} %get-tuple-element.17), channel_id=1, source_target_pairs={{0,1},{1,2},{2,3},{3,4},{4,5},{5,6},{6,7},{8,9},{9,10},{10,11},{11... | collective-permute-start | bytes 98312 | tf_op jit(solution)/shard_map/ppermute | solution.py:19
  103.3 6.1 %collective-permute-start.5 = (bf16[4,2,16,128]{3,2,1,0:T(8,128)(2,1)S(1)}, bf16[4,2,16,128]{3,2,1,0:T(8,128)(2,1)S(1)}, u32[]{:S(2)}, u32[]{:S(2)}) collective-permute-start(bf16[4,2,16,128]{3,2,1,0:T(8,128)(2,1)S(1)} %get-tuple-element.18), channel_id=1, source_target_pairs={{1,0},{2,1},{3,2},{4,3},{5,4},{6,5},{7,6},{9,8},{10,9},{11,10},{12... | collective-permute-start | bytes 98312 | tf_op jit(solution)/shard_map/ppermute | solution.py:21
  112.3 31.7 %copy-start.20 = (f32[8,16,128]{2,1,0:T(8,128)S(1)}, f32[8,16,128]{2,1,0:T(8,128)}, u32[]{:S(2)}) copy-start(f32[8,16,128]{2,1,0:T(8,128)} %param.6) | copy-start | bytes 196612
  112.3 44.1 %copy-start = (bf16[128,25,128]{0,1,2:T(8,128)(2,1)S(1)}, bf16[128,25,128]{0,1,2:T(8,128)(2,1)}, u32[]{:S(2)}) copy-start(bf16[128,25,128]{0,1,2:T(8,128)(2,1)} %fusion.4) | copy-start | bytes 2457604
  113.6 43.6 %copy-start.13 = (f32[8,16,128]{2,1,0:T(8,128)S(1)}, f32[8,16,128]{2,1,0:T(8,128)}, u32[]{:S(2)}) copy-start(f32[8,16,128]{2,1,0:T(8,128)} %fusion.281) | copy-start | bytes 196612
  113.6 43.6 %copy-start.19 = (f32[8,16,128]{2,1,0:T(8,128)S(1)}, f32[8,16,128]{2,1,0:T(8,128)}, u32[]{:S(2)}) copy-start(f32[8,16,128]{2,1,0:T(8,128)} %get-tuple-element.10) | copy-start | bytes 196612
  113.6 43.8 %copy-start.6 = (bf16[128,25,128]{0,1,2:T(8,128)(2,1)S(1)}, bf16[128,25,128]{0,1,2:T(8,128)(2,1)}, u32[]{:S(2)}) copy-start(bf16[128,25,128]{0,1,2:T(8,128)(2,1)} %fusion.5) | copy-start | bytes 2457604
  144.9 7.6 %collective-permute-start.6 = (bf16[2,16,128]{2,1,0:T(8,128)(2,1)S(1)}, bf16[2,16,128]{2,1,0:T(8,128)(2,1)S(1)}, u32[]{:S(2)}, u32[]{:S(2)}) collective-permute-start(bf16[2,16,128]{2,1,0:T(8,128)(2,1)S(1)} %get-tuple-element.21), channel_id=1, source_target_pairs={{0,1},{1,2},{2,3},{3,4},{4,5},{5,6},{6,7},{8,9},{9,10},{10,11},{11... | collective-permute-start | bytes 24584 | tf_op jit(solution)/shard_map/ppermute | solution.py:19
  150.5 5.9 %collective-permute-start.7 = (bf16[2,16,128]{2,1,0:T(8,128)(2,1)S(1)}, bf16[2,16,128]{2,1,0:T(8,128)(2,1)S(1)}, u32[]{:S(2)}, u32[]{:S(2)}) collective-permute-start(bf16[2,16,128]{2,1,0:T(8,128)(2,1)S(1)} %get-tuple-element.22), channel_id=1, source_target_pairs={{1,0},{2,1},{3,2},{4,3},{5,4},{6,5},{7,6},{9,8},{10,9},{11,10},{12... | collective-permute-start | bytes 24584 | tf_op jit(solution)/shard_map/ppermute | solution.py:21
  157.2 1.0 copy-start.11
  157.2 1.0 copy-start.18
  157.2 1.3 copy-start.4
  158.1 1.1 copy-start.9
  158.1 1.1 copy-start.17
  158.2 1.3 copy-start.2
  159.2 1.0 copy-start.15
  159.2 1.0 copy-start.16
Sparse Core Ops, SparseCore 0:
  48.1 33.1 all-reduce.6
  113.7 30.2 all-reduce.8
where the time goes:
time: 169 us; the launch traced here: 168 us
  waiting for transfers between devices  74.1 us (44%)
  matrix products  27.4 us (16%)
  starting transfers between devices  25.2 us (15%)
  other arithmetic  18 us (11%)
  between operations  14 us (8%)
  local copies, waits for them, and re-layouts  9.22 us (5%)
    psum x2, waiting for transfers between devices, shards(): sensor = lax.psum(partial_sensor, 'depth')  63.7 us
    ppermute x4, starting transfers between devices, with_halo(): lax.ppermute(tail, axis, [(i, (i + 1) % count) for i in range(ends)])  16.9 us
    dot_general x16, matrix products, project(): jnp.dot(flat_plane, dense, preferred_element_type=jnp.float32)  12.6 us
    ppermute x4, waiting for transfers between devices, with_halo(): lax.ppermute(head, axis, [((i + 1) % count, i) for i in range(ends)])  10.3 us
    ppermute x4, starting transfers between devices, with_halo(): lax.ppermute(head, axis, [((i + 1) % count, i) for i in range(ends)])  8.33 us
    convert_element_type x4, local copies, waits for them, and re-layouts, project(): dense = dense.astype(jnp.bfloat16).reshape(pixels, span_all * pixels)  7.6 us
    dot_general x4, matrix products, project(): jnp.einsum('ko,kji->ioj', one_hot, block_values, precision=lax.Precision....  6.06 us
    dot_general x4, matrix products, project(): jnp.einsum('ko,kji->joi', one_hot, block_values, precision=lax.Precision....  5.1 us
  transfers between devices with their start and end apart: 10, of which 5 were waited for; matrix products, arithmetic and copies ran while one was open for 18% of the time, Pallas kernels for 0%

commit v1 on v0

--- a/solution.py
+++ b/solution.py
@@ -101,7 +101,8 @@
                 shift_cols[plane_id],
                 False,
             )
-        sensor = lax.psum(partial_sensor, "depth")
+        pieces = lax.all_gather(partial_sensor, "depth")
+        sensor = jnp.sum(pieces, axis=0)
         ratio = (measured / sensor).astype(jnp.bfloat16)
         ratio_ext = with_halo(ratio, (("lat", 0),), RY)
         ratio_pad = jnp.pad(ratio_ext, ((0, 0), (RX, RX), (0, 0)))

time: 169 us -> 116 us (0.69)
  waiting for transfers between devices: 74.1 us -> 10.3 us
  blocking collectives: 0 us -> 25.6 us
  between operations: 14 us -> 0.61 us
    psum x2 -> x0, waiting for transfers between devices: 63.7 us -> none  [shards(): sensor = lax.psum(partial_sensor, 'depth')]
    all_gather x0 -> x2, blocking collectives: none -> 25.6 us  [shards(): pieces = lax.all_gather(partial_sensor, 'depth')]
  transfers between devices with their start and end apart: 10 -> 8, of which waited for: 5 -> 3; matrix products, arithmetic and copies ran while one was open for 18% -> 27% of each run, Pallas kernels for 0% -> 0%
where the time goes in v1:
time: 116 us; the launch traced here: 115 us
  matrix products  27.4 us (24%)
  blocking collectives  25.6 us (22%)
  starting transfers between devices  23.9 us (21%)
  other arithmetic  17.5 us (15%)
  waiting for transfers between devices  10.3 us (9%)
  local copies, waits for them, and re-layouts  9.22 us (8%)
    all_gather x2, blocking collectives, shards(): pieces = lax.all_gather(partial_sensor, 'depth')  25.6 us
    ppermute x4, starting transfers between devices, with_halo(): lax.ppermute(tail, axis, [(i, (i + 1) % count) for i in range(ends)])  15.6 us
    dot_general x16, matrix products, project(): jnp.dot(flat_plane, dense, preferred_element_type=jnp.float32)  12.7 us
    ppermute x4, waiting for transfers between devices, with_halo(): lax.ppermute(head, axis, [((i + 1) % count, i) for i in range(ends)])  10.3 us
    ppermute x4, starting transfers between devices, with_halo(): lax.ppermute(head, axis, [((i + 1) % count, i) for i in range(ends)])  8.33 us
    convert_element_type x4, local copies, waits for them, and re-layouts, project(): dense = dense.astype(jnp.bfloat16).reshape(pixels, span_all * pixels)  7.6 us
    dot_general x4, matrix products, project(): jnp.einsum('ko,kji->ioj', one_hot, block_values, precision=lax.Precision....  6.09 us
    dot_general x4, matrix products, project(): jnp.einsum('ko,kji->joi', one_hot, block_values, precision=lax.Precision....  5.12 us
  transfers between devices with their start and end apart: 8, of which 3 were waited for; matrix products, arithmetic and copies ran while one was open for 27% of the time, Pallas kernels for 0%

profile of v1, /device:TPU:3, one launch (start us, length us, event | category | flops | bytes accessed | tf_op | source)
XLA Modules:
  0.0 114.6 jit_solution(3182926670509095059)
XLA Ops:
  0.0 1.0 convert_element_type.60
  1.0 3.7 %collective-permute-start = (bf16[4,2,16,128]{3,2,1,0:T(8,128)(2,1)S(1)}, bf16[4,2,16,128]{3,2,1,0:T(8,128)(2,1)}, u32[]{:S(2)}, u32[]{:S(2)}) collective-permute-start(bf16[4,2,16,128]{3,2,1,0:T(8,128)(2,1)S(1)} %get-tuple-element.19), channel_id=1, source_target_pairs={{0,1},{1,2},{2,3},{3,4},{4,5},{5,6},{6,7},{8,9},{9,10},{10,11},{11... | collective-permute-start | bytes 98312 | tf_op jit(solution)/shard_map/ppermute | solution.py:19
  4.7 1.9 %collective-permute-start.1 = (bf16[4,2,16,128]{3,2,1,0:T(8,128)(2,1)S(1)}, bf16[4,2,16,128]{3,2,1,0:T(8,128)(2,1)}, u32[]{:S(2)}, u32[]{:S(2)}) collective-permute-start(bf16[4,2,16,128]{3,2,1,0:T(8,128)(2,1)S(1)} %get-tuple-element.20), channel_id=1, source_target_pairs={{1,0},{2,1},{3,2},{4,3},{5,4},{6,5},{7,6},{9,8},{10,9},{11,10},{12... | collective-permute-start | bytes 98312 | tf_op jit(solution)/shard_map/ppermute | solution.py:21
  8.8 2.5 %copy_select_fusion = bf16[4,13,128,128]{3,1,2,0:T(8,128)(2,1)S(1)} fusion(bf16[4,13,128,128]{3,2,1,0:T(8,128)(2,1)} %param.7, pred[4,13]{1,0:T(4,128)(4,1)S(1)} %iota_compare_fusion.12), kind=kLoop, calls=%fused_computation | loop fusion | flops 851968 | bytes 3407924 | tf_op jit(solution)/shard_map/jit(_where)/select_n | solution.py:75
  11.2 1.2 %convert_reduce_fusion.3 = (f32[13,128]{0,1:T(8,128)S(1)}, f32[13,128]{0,1:T(8,128)}, f32[13,128]{0,1:T(8,128)S(1)}, f32[13,128]{0,1:T(8,128)S(1)}) fusion(bf16[4,13,128,128]{3,1,2,0:T(8,128)(2,1)S(1)} %copy_select_fusion), kind=kLoop, calls=%fused_computation.20 | loop fusion | flops 1697280 | bytes 1730560 | tf_op jit(solution)/shard_map/reduce_sum | solution.py:87
  13.0 1.6 %fusion.2 = bf16[128,25,128]{2,1,0:T(8,128)(2,1)} fusion(bf16[4,13,128,128]{3,1,2,0:T(8,128)(2,1)S(1)} %copy_select_fusion, s32[13]{0:T(128)S(1)} %get-tuple-element.30), kind=kOutput, calls=%fused_computation.11 | convolution fusion | flops 11059525 | bytes 1344000 | tf_op jit(solution)/shard_map/ko,kji->joi/dot_general | solution.py:48
  14.6 1.5 %fusion.1 = bf16[128,25,128]{2,1,0:T(8,128)(2,1)} fusion(bf16[4,13,128,128]{3,1,2,0:T(8,128)(2,1)S(1)} %copy_select_fusion, s32[13]{0:T(128)S(1)} %get-tuple-element.32), kind=kOutput, calls=%fused_computation.10 | convolution fusion | flops 11059525 | bytes 1344000 | tf_op jit(solution)/shard_map/ko,kji->joi/dot_general | solution.py:48
  16.1 1.5 %fusion = bf16[128,25,128]{2,1,0:T(8,128)(2,1)} fusion(bf16[4,13,128,128]{3,1,2,0:T(8,128)(2,1)S(1)} %copy_select_fusion, s32[13]{0:T(128)S(1)} %get-tuple-element.34), kind=kOutput, calls=%fused_computation.9 | convolution fusion | flops 11059525 | bytes 1344000 | tf_op jit(solution)/shard_map/ko,kji->joi/dot_general | solution.py:48
  17.6 1.5 %fusion.4 = bf16[128,25,128]{0,1,2:T(8,128)(2,1)} fusion(bf16[4,13,128,128]{3,1,2,0:T(8,128)(2,1)S(1)} %copy_select_fusion, s32[13]{0:T(128)S(1)} %get-tuple-element.27), kind=kOutput, calls=%fused_computation.13 | convolution fusion | flops 11059525 | bytes 1344000 | tf_op jit(solution)/shard_map/ko,kji->ioj/dot_general | solution.py:46
  19.8 1.5 %fusion.5 = bf16[128,25,128]{0,1,2:T(8,128)(2,1)} fusion(bf16[4,13,128,128]{3,1,2,0:T(8,128)(2,1)S(1)} %copy_select_fusion, s32[13]{0:T(128)S(1)} %get-tuple-element.33), kind=kOutput, calls=%fused_computation.14 | convolution fusion | flops 11059525 | bytes 1344000 | tf_op jit(solution)/shard_map/ko,kji->ioj/dot_general | solution.py:46
  21.9 1.5 %fusion.6 = bf16[128,25,128]{0,1,2:T(8,128)(2,1)} fusion(bf16[4,13,128,128]{3,1,2,0:T(8,128)(2,1)S(1)} %copy_select_fusion, s32[13]{0:T(128)S(1)} %get-tuple-element.31), kind=kOutput, calls=%fused_computation.15 | convolution fusion | flops 11059525 | bytes 1344000 | tf_op jit(solution)/shard_map/ko,kji->ioj/dot_general | solution.py:46
  24.1 1.5 %fusion.7 = bf16[128,25,128]{0,1,2:T(8,128)(2,1)} fusion(bf16[4,13,128,128]{3,1,2,0:T(8,128)(2,1)S(1)} %copy_select_fusion, s32[13]{0:T(128)S(1)} %get-tuple-element.29), kind=kOutput, calls=%fused_computation.16 | convolution fusion | flops 11059525 | bytes 1344000 | tf_op jit(solution)/shard_map/ko,kji->ioj/dot_general | solution.py:46
  28.9 1.2 %copy.892 = bf16[128,25,128]{0,2,1:T(8,128)(2,1)S(1)} copy(bf16[128,25,128]{2,1,0:T(8,128)(2,1)S(1)} %fusion.3) | data formatting | bytes 1638400 | tf_op jit(solution)/shard_map/convert_element_type | solution.py:49
  30.0 2.1 %copy.866 = bf16[128,25,128]{0,2,1:T(8,128)(2,1)S(1)} copy(bf16[128,25,128]{2,1,0:T(8,128)(2,1)} %fusion.2) | data formatting | bytes 1638400 | tf_op jit(solution)/shard_map/convert_element_type | solution.py:49
  32.2 2.1 %copy.840 = bf16[128,25,128]{0,2,1:T(8,128)(2,1)S(1)} copy(bf16[128,25,128]{2,1,0:T(8,128)(2,1)} %fusion.1) | data formatting | bytes 1638400 | tf_op jit(solution)/shard_map/convert_element_type | solution.py:49
  34.4 2.1 %copy.815 = bf16[128,25,128]{0,2,1:T(8,128)(2,1)S(1)} copy(bf16[128,25,128]{2,1,0:T(8,128)(2,1)} %fusion) | data formatting | bytes 1638400 | tf_op jit(solution)/shard_map/convert_element_type | solution.py:49
  36.5 0.9 select_maximum_fusion.5
  40.8 13.2 %all_gather.8 = f32[4,8,16,128]{3,2,1,0:T(8,128)} all-gather(f32[1,8,16,128]{3,2,1,0:T(8,128)S(1)} %fusion.221), channel_id=1, replica_groups=mesh['depth'=4,'lat'=8] {'depth'}, dimensions={0}, use_global_device_ids=true | all-gather | bytes 327680 | tf_op jit(solution)/shard_map/all_gather | solution.py:104
  54.0 1.6 %reduce_sum.54 = f32[8,16,128]{2,1,0:T(8,128)} reduce(f32[4,8,16,128]{3,2,1,0:T(8,128)} %all_gather.8, f32[]{:T(128)} %constant.48.clone.1), dimensions={0}, to_apply=%region_0.1 | reduce | flops 49152 | bytes 327684 | tf_op jit(solution)/shard_map/reduce_sum | solution.py:105
  55.6 1.0 divide_convert_fusion.1
  56.6 6.3 %collective-permute-start.2 = (bf16[2,16,128]{2,1,0:T(8,128)(2,1)S(1)}, bf16[2,16,128]{2,1,0:T(8,128)(2,1)S(1)}, u32[]{:S(2)}, u32[]{:S(2)}) collective-permute-start(bf16[2,16,128]{2,1,0:T(8,128)(2,1)S(1)} %get-tuple-element.23), channel_id=1, source_target_pairs={{0,1},{1,2},{2,3},{3,4},{4,5},{5,6},{6,7},{8,9},{9,10},{10,11},{11... | collective-permute-start | bytes 24584 | tf_op jit(solution)/shard_map/ppermute | solution.py:19
  62.9 2.1 %collective-permute-start.3 = (bf16[2,16,128]{2,1,0:T(8,128)(2,1)S(1)}, bf16[2,16,128]{2,1,0:T(8,128)(2,1)S(1)}, u32[]{:S(2)}, u32[]{:S(2)}) collective-permute-start(bf16[2,16,128]{2,1,0:T(8,128)(2,1)S(1)} %get-tuple-element.24), channel_id=1, source_target_pairs={{1,0},{2,1},{3,2},{4,3},{5,4},{6,5},{7,6},{9,8},{10,9},{11,10},{12... | collective-permute-start | bytes 24584 | tf_op jit(solution)/shard_map/ppermute | solution.py:21
  65.1 1.1 fusion.275
  66.1 2.7 %collective-permute-done.3 = bf16[2,16,128]{2,1,0:T(8,128)(2,1)S(1)} collective-permute-done((bf16[2,16,128]{2,1,0:T(8,128)(2,1)S(1)}, bf16[2,16,128]{2,1,0:T(8,128)(2,1)S(1)}, u32[]{:S(2)}, u32[]{:S(2)}) %collective-permute-start.3) | collective-permute-done | bytes 8224 | tf_op jit(solution)/shard_map/ppermute | solution.py:21
  68.8 2.0 %fusion.22 = f32[12,20,25,128]{3,1,2,0:T(8,128)S(1)} fusion(bf16[128,25,128]{0,1,2:T(8,128)(2,1)} %fusion.4, bf16[2,16,128]{2,1,0:T(8,128)(2,1)S(1)} %collective-permute-done.3, bf16[8,16,128]{2,1,0:T(8,128)(2,1)S(1)} %divide_convert_fusion.1, bf16[2,16,128]{2,1,0:T(8,128)(2,1)S(1)} %collective-permute-done.2), kind=kOutput, calls=%fused_computation.37 | convolution fusion | flops 196976640 | bytes 3940352 | tf_op jit(solution)/shard_map/dot_general | solution.py:50
  76.3 1.9 %collective-permute-start.4 = (bf16[4,2,16,128]{3,2,1,0:T(8,128)(2,1)S(1)}, bf16[4,2,16,128]{3,2,1,0:T(8,128)(2,1)S(1)}, u32[]{:S(2)}, u32[]{:S(2)}) collective-permute-start(bf16[4,2,16,128]{3,2,1,0:T(8,128)(2,1)S(1)} %get-tuple-element.17), channel_id=1, source_target_pairs={{0,1},{1,2},{2,3},{3,4},{4,5},{5,6},{6,7},{8,9},{9,10},{10,11},{11... | collective-permute-start | bytes 98312 | tf_op jit(solution)/shard_map/ppermute | solution.py:19
  78.3 2.4 %collective-permute-start.5 = (bf16[4,2,16,128]{3,2,1,0:T(8,128)(2,1)S(1)}, bf16[4,2,16,128]{3,2,1,0:T(8,128)(2,1)S(1)}, u32[]{:S(2)}, u32[]{:S(2)}) collective-permute-start(bf16[4,2,16,128]{3,2,1,0:T(8,128)(2,1)S(1)} %get-tuple-element.18), channel_id=1, source_target_pairs={{1,0},{2,1},{3,2},{4,3},{5,4},{6,5},{7,6},{9,8},{10,9},{11,10},{12... | collective-permute-start | bytes 98312 | tf_op jit(solution)/shard_map/ppermute | solution.py:21
  80.7 3.7 %collective-permute-done.5 = bf16[4,2,16,128]{3,2,1,0:T(8,128)(2,1)S(1)} collective-permute-done((bf16[4,2,16,128]{3,2,1,0:T(8,128)(2,1)S(1)}, bf16[4,2,16,128]{3,2,1,0:T(8,128)(2,1)S(1)}, u32[]{:S(2)}, u32[]{:S(2)}) %collective-permute-start.5) | collective-permute-done | bytes 32800 | tf_op jit(solution)/shard_map/ppermute | solution.py:21
  88.0 12.3 %all_gather.9 = f32[4,8,16,128]{3,2,1,0:T(8,128)S(1)} all-gather(f32[1,8,16,128]{3,2,1,0:T(8,128)S(1)} %fusion.106), channel_id=1, replica_groups=mesh['depth'=4,'lat'=8] {'depth'}, dimensions={0}, use_global_device_ids=true | all-gather | bytes 327680 | tf_op jit(solution)/shard_map/all_gather | solution.py:104
  100.4 3.6 %collective-permute-start.6 = (bf16[2,16,128]{2,1,0:T(8,128)(2,1)S(1)}, bf16[2,16,128]{2,1,0:T(8,128)(2,1)S(1)}, u32[]{:S(2)}, u32[]{:S(2)}) collective-permute-start(bf16[2,16,128]{2,1,0:T(8,128)(2,1)S(1)} %get-tuple-element.21), channel_id=1, source_target_pairs={{0,1},{1,2},{2,3},{3,4},{4,5},{5,6},{6,7},{8,9},{9,10},{10,11},{11... | collective-permute-start | bytes 24584 | tf_op jit(solution)/shard_map/ppermute | solution.py:19
  104.0 1.9 %collective-permute-start.7 = (bf16[2,16,128]{2,1,0:T(8,128)(2,1)S(1)}, bf16[2,16,128]{2,1,0:T(8,128)(2,1)S(1)}, u32[]{:S(2)}, u32[]{:S(2)}) collective-permute-start(bf16[2,16,128]{2,1,0:T(8,128)(2,1)S(1)} %get-tuple-element.22), channel_id=1, source_target_pairs={{1,0},{2,1},{3,2},{4,3},{5,4},{6,5},{7,6},{9,8},{10,9},{11,10},{12... | collective-permute-start | bytes 24584 | tf_op jit(solution)/shard_map/ppermute | solution.py:21
  106.0 3.9 %collective-permute-done.7 = bf16[2,16,128]{2,1,0:T(8,128)(2,1)S(1)} collective-permute-done((bf16[2,16,128]{2,1,0:T(8,128)(2,1)S(1)}, bf16[2,16,128]{2,1,0:T(8,128)(2,1)S(1)}, u32[]{:S(2)}, u32[]{:S(2)}) %collective-permute-start.7) | collective-permute-done | bytes 8224 | tf_op jit(solution)/shard_map/ppermute | solution.py:21
  (95 shorter events, 24.8 us)
Async XLA Ops:
  1.0 35.5 %collective-permute-start = (bf16[4,2,16,128]{3,2,1,0:T(8,128)(2,1)S(1)}, bf16[4,2,16,128]{3,2,1,0:T(8,128)(2,1)}, u32[]{:S(2)}, u32[]{:S(2)}) collective-permute-start(bf16[4,2,16,128]{3,2,1,0:T(8,128)(2,1)S(1)} %get-tuple-element.19), channel_id=1, source_target_pairs={{0,1},{1,2},{2,3},{3,4},{4,5},{5,6},{6,7},{8,9},{9,10},{10,11},{11... | collective-permute-start | bytes 98312 | tf_op jit(solution)/shard_map/ppermute | solution.py:19
  4.7 31.8 %collective-permute-start.1 = (bf16[4,2,16,128]{3,2,1,0:T(8,128)(2,1)S(1)}, bf16[4,2,16,128]{3,2,1,0:T(8,128)(2,1)}, u32[]{:S(2)}, u32[]{:S(2)}) collective-permute-start(bf16[4,2,16,128]{3,2,1,0:T(8,128)(2,1)S(1)} %get-tuple-element.20), channel_id=1, source_target_pairs={{1,0},{2,1},{3,2},{4,3},{5,4},{6,5},{7,6},{9,8},{10,9},{11,10},{12... | collective-permute-start | bytes 98312 | tf_op jit(solution)/shard_map/ppermute | solution.py:21
  40.8 30.0 %copy-start.7 = (f32[4,8,16,128]{3,2,1,0:T(8,128)S(1)}, f32[4,8,16,128]{3,2,1,0:T(8,128)}, u32[]{:S(2)}) copy-start(f32[4,8,16,128]{3,2,1,0:T(8,128)} %param.5) | copy-start | bytes 786436
  55.6 15.2 %copy-start.12 = (f32[8,16,128]{2,1,0:T(8,128)S(1)}, f32[8,16,128]{2,1,0:T(8,128)}, u32[]{:S(2)}) copy-start(f32[8,16,128]{2,1,0:T(8,128)} %fusion.281) | copy-start | bytes 196612
  55.6 16.0 %copy-start.5 = (bf16[128,25,128]{0,1,2:T(8,128)(2,1)S(1)}, bf16[128,25,128]{0,1,2:T(8,128)(2,1)}, u32[]{:S(2)}) copy-start(bf16[128,25,128]{0,1,2:T(8,128)(2,1)} %fusion.5) | copy-start | bytes 2457604
  56.6 9.5 %collective-permute-start.2 = (bf16[2,16,128]{2,1,0:T(8,128)(2,1)S(1)}, bf16[2,16,128]{2,1,0:T(8,128)(2,1)S(1)}, u32[]{:S(2)}, u32[]{:S(2)}) collective-permute-start(bf16[2,16,128]{2,1,0:T(8,128)(2,1)S(1)} %get-tuple-element.23), channel_id=1, source_target_pairs={{0,1},{1,2},{2,3},{3,4},{4,5},{5,6},{6,7},{8,9},{9,10},{10,11},{11... | collective-permute-start | bytes 24584 | tf_op jit(solution)/shard_map/ppermute | solution.py:19
  62.9 5.9 %collective-permute-start.3 = (bf16[2,16,128]{2,1,0:T(8,128)(2,1)S(1)}, bf16[2,16,128]{2,1,0:T(8,128)(2,1)S(1)}, u32[]{:S(2)}, u32[]{:S(2)}) collective-permute-start(bf16[2,16,128]{2,1,0:T(8,128)(2,1)S(1)} %get-tuple-element.24), channel_id=1, source_target_pairs={{1,0},{2,1},{3,2},{4,3},{5,4},{6,5},{7,6},{9,8},{10,9},{11,10},{12... | collective-permute-start | bytes 24584 | tf_op jit(solution)/shard_map/ppermute | solution.py:21
  66.1 9.4 %copy-start.14 = (f32[8,16,128]{2,1,0:T(8,128)}, f32[8,16,128]{2,1,0:T(8,128)S(1)}, u32[]{:S(2)}) copy-start(f32[8,16,128]{2,1,0:T(8,128)S(1)} %fusion.275) | copy-start | bytes 196612
  70.8 1.6 %copy-start.10 = (f32[8,16,128]{2,1,0:T(8,128)S(1)}, f32[8,16,128]{2,1,0:T(8,128)}, u32[]{:S(2)}) copy-start(f32[8,16,128]{2,1,0:T(8,128)} %fusion.279) | copy-start | bytes 196612
  70.8 2.4 %copy-start.3 = (bf16[128,25,128]{0,1,2:T(8,128)(2,1)S(1)}, bf16[128,25,128]{0,1,2:T(8,128)(2,1)}, u32[]{:S(2)}) copy-start(bf16[128,25,128]{0,1,2:T(8,128)(2,1)} %fusion.6) | copy-start | bytes 2457604
  72.4 1.6 %copy-start.8 = (f32[8,16,128]{2,1,0:T(8,128)S(1)}, f32[8,16,128]{2,1,0:T(8,128)}, u32[]{:S(2)}) copy-start(f32[8,16,128]{2,1,0:T(8,128)} %fusion.277) | copy-start | bytes 196612
  72.4 2.4 %copy-start.1 = (bf16[128,25,128]{0,1,2:T(8,128)(2,1)S(1)}, bf16[128,25,128]{0,1,2:T(8,128)(2,1)}, u32[]{:S(2)}) copy-start(bf16[128,25,128]{0,1,2:T(8,128)(2,1)} %fusion.7) | copy-start | bytes 2457604
  76.3 4.3 %collective-permute-start.4 = (bf16[4,2,16,128]{3,2,1,0:T(8,128)(2,1)S(1)}, bf16[4,2,16,128]{3,2,1,0:T(8,128)(2,1)S(1)}, u32[]{:S(2)}, u32[]{:S(2)}) collective-permute-start(bf16[4,2,16,128]{3,2,1,0:T(8,128)(2,1)S(1)} %get-tuple-element.17), channel_id=1, source_target_pairs={{0,1},{1,2},{2,3},{3,4},{4,5},{5,6},{6,7},{8,9},{9,10},{10,11},{11... | collective-permute-start | bytes 98312 | tf_op jit(solution)/shard_map/ppermute | solution.py:19
  78.3 6.1 %collective-permute-start.5 = (bf16[4,2,16,128]{3,2,1,0:T(8,128)(2,1)S(1)}, bf16[4,2,16,128]{3,2,1,0:T(8,128)(2,1)S(1)}, u32[]{:S(2)}, u32[]{:S(2)}) collective-permute-start(bf16[4,2,16,128]{3,2,1,0:T(8,128)(2,1)S(1)} %get-tuple-element.18), channel_id=1, source_target_pairs={{1,0},{2,1},{3,2},{4,3},{5,4},{6,5},{7,6},{9,8},{10,9},{11,10},{12... | collective-permute-start | bytes 98312 | tf_op jit(solution)/shard_map/ppermute | solution.py:21
  87.3 13.0 %copy-start.20 = (f32[8,16,128]{2,1,0:T(8,128)S(1)}, f32[8,16,128]{2,1,0:T(8,128)}, u32[]{:S(2)}) copy-start(f32[8,16,128]{2,1,0:T(8,128)} %param.6) | copy-start | bytes 196612
  87.3 22.6 %copy-start = (bf16[128,25,128]{0,1,2:T(8,128)(2,1)S(1)}, bf16[128,25,128]{0,1,2:T(8,128)(2,1)}, u32[]{:S(2)}) copy-start(bf16[128,25,128]{0,1,2:T(8,128)(2,1)} %fusion.4) | copy-start | bytes 2457604
  87.9 22.7 %copy-start.13 = (f32[8,16,128]{2,1,0:T(8,128)S(1)}, f32[8,16,128]{2,1,0:T(8,128)}, u32[]{:S(2)}) copy-start(f32[8,16,128]{2,1,0:T(8,128)} %fusion.281) | copy-start | bytes 196612
  87.9 22.7 %copy-start.19 = (f32[8,16,128]{2,1,0:T(8,128)S(1)}, f32[8,16,128]{2,1,0:T(8,128)}, u32[]{:S(2)}) copy-start(f32[8,16,128]{2,1,0:T(8,128)} %get-tuple-element.10) | copy-start | bytes 196612
  88.0 22.9 %copy-start.6 = (bf16[128,25,128]{0,1,2:T(8,128)(2,1)S(1)}, bf16[128,25,128]{0,1,2:T(8,128)(2,1)}, u32[]{:S(2)}) copy-start(bf16[128,25,128]{0,1,2:T(8,128)(2,1)} %fusion.5) | copy-start | bytes 2457604
  100.4 5.6 %collective-permute-start.6 = (bf16[2,16,128]{2,1,0:T(8,128)(2,1)S(1)}, bf16[2,16,128]{2,1,0:T(8,128)(2,1)S(1)}, u32[]{:S(2)}, u32[]{:S(2)}) collective-permute-start(bf16[2,16,128]{2,1,0:T(8,128)(2,1)S(1)} %get-tuple-element.21), channel_id=1, source_target_pairs={{0,1},{1,2},{2,3},{3,4},{4,5},{5,6},{6,7},{8,9},{9,10},{10,11},{11... | collective-permute-start | bytes 24584 | tf_op jit(solution)/shard_map/ppermute | solution.py:19
  104.0 5.9 %collective-permute-start.7 = (bf16[2,16,128]{2,1,0:T(8,128)(2,1)S(1)}, bf16[2,16,128]{2,1,0:T(8,128)(2,1)S(1)}, u32[]{:S(2)}, u32[]{:S(2)}) collective-permute-start(bf16[2,16,128]{2,1,0:T(8,128)(2,1)S(1)} %get-tuple-element.22), channel_id=1, source_target_pairs={{1,0},{2,1},{3,2},{4,3},{5,4},{6,5},{7,6},{9,8},{10,9},{11,10},{12... | collective-permute-start | bytes 24584 | tf_op jit(solution)/shard_map/ppermute | solution.py:21
  110.6 1.0 copy-start.11
  110.7 1.0 copy-start.18
  110.7 1.3 %copy-start.4 = (bf16[128,25,128]{0,1,2:T(8,128)(2,1)S(1)}, bf16[128,25,128]{0,1,2:T(8,128)(2,1)}, u32[]{:S(2)}) copy-start(bf16[128,25,128]{0,1,2:T(8,128)(2,1)} %fusion.6) | copy-start | bytes 2457604
  111.6 1.1 copy-start.9
  111.6 1.1 copy-start.17
  111.7 1.3 %copy-start.2 = (bf16[128,25,128]{0,1,2:T(8,128)(2,1)S(1)}, bf16[128,25,128]{0,1,2:T(8,128)(2,1)}, u32[]{:S(2)}) copy-start(bf16[128,25,128]{0,1,2:T(8,128)(2,1)} %fusion.7) | copy-start | bytes 2457604
  112.7 1.0 copy-start.15
  112.7 1.0 copy-start.16
